TPU v7x, 32 devices: a whole 2x2x4 slice. The times are simulated.
32 devices in a mesh: gx: 4 (over y, x), gy: 8 (over z, core).
Axes of the slice: x: 2, y: 2, z: 4, core: 2. Of those that a mesh axis runs over, the one named last changes fastest.
Arguments:
- populations: float32 [19, 128, 64, 256], P(None, 'gx', 'gy'), may hold values from 0.02 to 0.08
- mass: float32 [256, 1024], P('gx', 'gy'), may hold values from 0.2 to 1
- modulus: float32 [256, 1024], P('gx', 'gy'), may hold values from 0.1 to 0.5
- cell_live: int32 [256, 1024], P('gx', 'gy'), may hold values 0 or 1
- stiff_ref: float32 [12, 12], replicated, as said below
- rec_block: int32 [131072], P(('gx', 'gy')), may hold values from 0 to 255
- rec_owner: int32 [131072, 1], P(('gx', 'gy')), may hold values from 0 to 31; in each aligned block of 4096 rows (0 to 4095, 4096 to 8191, ...) at most 256 rows name the same one
- rec_node: int32 [131072], P(('gx', 'gy')), may hold values from 0 to 8191
- rbf_weight: float32 [131072, 256], P(('gx', 'gy')), may hold values from 0 to 2
Outputs:
- populations_next: float32 [19, 128, 64, 256], P(None, 'gx', 'gy')
- displacement: float32 [3, 256, 1024], P(None, 'gx', 'gy')
Inputs may be any that keep to these rules, and one draw needn't show every extreme that they name: `rec_owner`: in the records of one device no owner is named more than 256 times, and every owner is named by some record. `stiff_ref`: symmetric with a positive diagonal that exceeds the sum of magnitudes of each row's other entries.
All inputs are finite; a program needn't handle non-finite values. No bound on the sum of `cell_live` on one device may be relied on, other than what follows from the above.
Results may differ from a plain program's by a relative error of at most 0.0003.
Values sent between devices are 32-bit elements; how exact they have to be, the bound alone decides.
A program may use at most 128 MiB of HBM per device.

v0:
```python
import functools

import jax
import jax.numpy as jnp
from jax import lax
from jax.experimental import pallas as pl
from jax.experimental.pallas import tpu as pltpu
from jax.sharding import PartitionSpec as P

MESH = pl.DeviceIdType.MESH
F32 = jnp.float32
BF16 = jnp.bfloat16
LANES = 128

lattice_dirs = (
    (0, 0, 0),
    (1, 0, 0),
    (-1, 0, 0),
    (0, 1, 0),
    (0, -1, 0),
    (0, 0, 1),
    (0, 0, -1),
    (1, 1, 0),
    (-1, -1, 0),
    (1, -1, 0),
    (-1, 1, 0),
    (1, 0, 1),
    (-1, 0, -1),
    (1, 0, -1),
    (-1, 0, 1),
    (0, 1, 1),
    (0, -1, -1),
    (0, 1, -1),
    (0, -1, 1),
)
lattice_weights = (1.0 / 3.0,) + (1.0 / 18.0,) * 6 + (1.0 / 36.0,) * 12
relax_rate = 1.25
coupling = 0.1

x_up = [q for q in range(19) if lattice_dirs[q][0] == 1]
x_down = [q for q in range(19) if lattice_dirs[q][0] == -1]
y_up = [q for q in range(19) if lattice_dirs[q][1] == 1]
y_down = [q for q in range(19) if lattice_dirs[q][1] == -1]
diagonal = [q for q in range(19) if lattice_dirs[q][0] != 0 and lattice_dirs[q][1] != 0]


def combine_dirs(fields, direction):
    total = None
    for axis_pos in range(3):
        if direction[axis_pos] != 0:
            field = fields[axis_pos]
            if total is None:
                total = field if direction[axis_pos] == 1 else -field
            else:
                total = total + field if direction[axis_pos] == 1 else total - field
    return total


def halves(values):
    high = values.astype(BF16)
    low = (values - high.astype(F32)).astype(BF16)
    return high, low


def iota(shape, dim):
    return lax.broadcasted_iota(jnp.int32, shape, dim)


def dot_nt(left, right):
    return lax.dot_general(left, right, (((1,), (1,)), ((), ())), preferred_element_type=F32)


def dot_nn(left, right):
    return lax.dot_general(left, right, (((1,), (0,)), ((), ())), preferred_element_type=F32)


def collide_kernel(pop_ref, relaxed_ref, moment_ref, xu_ref, xd_ref, yu_ref, yd_ref):
    step = pl.program_id(0)
    last = pl.num_programs(0) - 1
    rows, cols, depth = pop_ref.shape[1:]

    def one(row, carry):
        pops = [pop_ref[q, row] for q in range(19)]
        density = pops[0]
        for q in range(1, 19):
            density = density + pops[q]
        moment = []
        for axis_pos in range(3):
            total = None
            for q in range(19):
                sign = lattice_dirs[q][axis_pos]
                if sign == 1:
                    total = pops[q] if total is None else total + pops[q]
                elif sign == -1:
                    total = -pops[q] if total is None else total - pops[q]
            moment.append(total)
            moment_ref[axis_pos, row] = total
        velocity = [moment[axis_pos] / density for axis_pos in range(3)]
        squared = (
            velocity[0] * velocity[0] + velocity[1] * velocity[1] + velocity[2] * velocity[2]
        )
        rest = 1.0 - 1.5 * squared
        for q in range(19):
            projected = combine_dirs(velocity, lattice_dirs[q])
            bracket = rest
            if projected is not None:
                bracket = rest + projected * (3.0 + 4.5 * projected)
            relaxed = (1.0 - relax_rate) * pops[q] + (
                relax_rate * lattice_weights[q]
            ) * density * bracket
            relaxed_ref[q, row] = relaxed
            if q in y_up:
                yu_ref[y_up.index(q), row] = relaxed[cols - 1 : cols]
            if q in y_down:
                yd_ref[y_down.index(q), row] = relaxed[0:1]
        return carry

    lax.fori_loop(0, rows, one, 0)

    @pl.when(step == 0)
    def _():
        for k, q in enumerate(x_down):
            xd_ref[k] = relaxed_ref[q, 0]

    @pl.when(step == last)
    def _():
        for k, q in enumerate(x_up):
            xu_ref[k] = relaxed_ref[q, rows - 1]


def collide(populations):
    _, nx, ny, nz = populations.shape
    rows = 8
    steps = nx // rows
    return pl.pallas_call(
        collide_kernel,
        grid=(steps,),
        in_specs=[pl.BlockSpec((19, rows, ny, nz), lambda i: (0, i, 0, 0))],
        out_specs=[
            pl.BlockSpec((19, rows, ny, nz), lambda i: (0, i, 0, 0)),
            pl.BlockSpec((3, rows, ny, nz), lambda i: (0, i, 0, 0)),
            pl.BlockSpec((5, ny, nz), lambda i: (0, 0, 0)),
            pl.BlockSpec((5, ny, nz), lambda i: (0, 0, 0)),
            pl.BlockSpec((5, rows, 1, nz), lambda i: (0, i, 0, 0)),
            pl.BlockSpec((5, rows, 1, nz), lambda i: (0, i, 0, 0)),
        ],
        out_shape=[
            jax.ShapeDtypeStruct((19, nx, ny, nz), F32),
            jax.ShapeDtypeStruct((3, nx, ny, nz), F32),
            jax.ShapeDtypeStruct((5, ny, nz), F32),
            jax.ShapeDtypeStruct((5, ny, nz), F32),
            jax.ShapeDtypeStruct((5, nx, 1, nz), F32),
            jax.ShapeDtypeStruct((5, nx, 1, nz), F32),
        ],
        compiler_params=pltpu.CompilerParams(dimension_semantics=("arbitrary",)),
        name="collide",
    )(populations)


def pack_kernel(
    devices, parts, node_cols, mom_ref, w_ref, blk_ref, own_ref, node_ref,
    out_ref, slot_ref, mom_cat, tri, base, acc,
):
    step = pl.program_id(0)
    blocks = mom_ref.shape[0] // 3
    chunk = w_ref.shape[0]

    @pl.when(step == 0)
    def _():
        high, low = halves(mom_ref[...])
        mom_cat[...] = jnp.concatenate([high, low, high], axis=1)
        before = iota((chunk, chunk), 0) <= iota((chunk, chunk), 1)
        tri[...] = before.astype(F32).astype(BF16)
        base[...] = jnp.zeros_like(base)
        acc[...] = jnp.zeros_like(acc)

    w_high, w_low = halves(w_ref[...])
    products = dot_nt(mom_cat[...], jnp.concatenate([w_high, w_high, w_low], axis=1))
    here = iota((blocks, chunk), 0) == blk_ref[...]
    loads = [
        jnp.sum(
            jnp.where(here, products[c * blocks : (c + 1) * blocks], 0.0), axis=0, keepdims=True
        )
        for c in range(3)
    ]
    owners = own_ref[...]
    hits = (iota((devices, chunk), 0) == owners).astype(F32)
    counts = dot_nn(hits.astype(BF16), tri[...])
    slots = jnp.sum(hits * (counts - 1.0 + base[:, 0:1]), axis=0, keepdims=True)
    base[...] = base[...] + counts[:, chunk - 1 : chunk]
    slot_id = slots.astype(jnp.int32)
    slot_ref[...] = slot_id
    part = slot_id // LANES
    place = slot_id - part * LANES
    node = node_ref[...]
    node_row = node // node_cols
    node_high = (node_row * node_cols).astype(F32)
    node_low = (node - node_row * node_cols).astype(F32)
    channel = iota((8, chunk), 0) // parts
    in_part = (iota((8, chunk), 0) - channel * parts) == part
    high_rows = jnp.zeros((8, chunk), F32)
    low_rows = jnp.zeros((8, chunk), F32)
    for c in range(4):
        if c < 3:
            high = loads[c].astype(BF16).astype(F32)
            low = loads[c] - high
        else:
            high, low = node_high, node_low
        high_rows = jnp.where(in_part & (channel == c), high, high_rows)
        low_rows = jnp.where(in_part & (channel == c), low, low_rows)
    mine = (iota((devices * 8, chunk), 0) // 8) == owners

    def spread(rows):
        tiled = jnp.broadcast_to(rows[None], (devices, 8, chunk)).reshape(devices * 8, chunk)
        return jnp.where(mine, tiled, 0.0).astype(BF16)

    slot_hot = (iota((LANES, chunk), 0) == place).astype(F32).astype(BF16)
    acc[...] += dot_nt(
        jnp.concatenate([spread(high_rows), spread(low_rows)], axis=1),
        jnp.concatenate([slot_hot, slot_hot], axis=1),
    )

    @pl.when(step == pl.num_programs(0) - 1)
    def _():
        out_ref[...] = acc[...].reshape(devices, 8, LANES)


def pack_loads(devices, parts, node_cols, moment, weights, blk, own, node):
    records, depth = weights.shape
    chunk = 512
    rows3 = moment.shape[0]
    row_spec = pl.BlockSpec((1, chunk), lambda i: (0, i))
    return pl.pallas_call(
        functools.partial(pack_kernel, devices, parts, node_cols),
        grid=(records // chunk,),
        in_specs=[
            pl.BlockSpec((rows3, depth), lambda i: (0, 0)),
            pl.BlockSpec((chunk, depth), lambda i: (i, 0)),
            row_spec,
            row_spec,
            row_spec,
        ],
        out_specs=[
            pl.BlockSpec((devices, 8, LANES), lambda i: (0, 0, 0)),
            row_spec,
        ],
        out_shape=[
            jax.ShapeDtypeStruct((devices, 8, LANES), F32),
            jax.ShapeDtypeStruct((1, records), jnp.int32),
        ],
        scratch_shapes=[
            pltpu.VMEM((rows3, 3 * depth), BF16),
            pltpu.VMEM((chunk, chunk), BF16),
            pltpu.VMEM((devices, LANES), F32),
            pltpu.VMEM((devices * 8, LANES), F32),
        ],
        compiler_params=pltpu.CompilerParams(dimension_semantics=("arbitrary",)),
        name="pack_loads",
    )(moment, weights, blk, own, node)


def position(grid):
    return lax.axis_index("gx"), lax.axis_index("gy")


def greet_all(grid):
    ix, iy = position(grid)
    devices = grid[0] * grid[1]
    me = ix * grid[1] + iy
    barrier = pltpu.get_barrier_semaphore()

    def signal(j, carry):
        other = lax.rem(me + j, devices)
        pl.semaphore_signal(
            barrier, inc=1, device_id=(other // grid[1], lax.rem(other, grid[1])),
            device_id_type=MESH,
        )
        return carry

    lax.fori_loop(1, devices, signal, 0)
    pl.semaphore_wait(barrier, devices - 1)


def broadcast_copy(grid, j, source, target, send_sem, recv_sem):
    ix, iy = position(grid)
    devices = grid[0] * grid[1]
    me = ix * grid[1] + iy
    other = lax.rem(me + j, devices)
    return pltpu.make_async_remote_copy(
        src_ref=source(other),
        dst_ref=target(me),
        send_sem=send_sem.at[j],
        recv_sem=recv_sem.at[j],
        device_id=(other // grid[1], lax.rem(other, grid[1])),
        device_id_type=MESH,
    )


def to_all(grid, source, target, send_sem, recv_sem, start):
    def body(j, carry):
        copy = broadcast_copy(grid, j, source, target, send_sem, recv_sem)
        if start:
            copy.start()
        else:
            copy.wait()
        return carry

    lax.fori_loop(1, grid[0] * grid[1], body, 0)


def neighbour_copy(grid, dx, dy, source, target, send_sem, recv_sem):
    ix, iy = position(grid)
    return pltpu.make_async_remote_copy(
        src_ref=source,
        dst_ref=target,
        send_sem=send_sem,
        recv_sem=recv_sem,
        device_id=(lax.rem(ix + dx + grid[0], grid[0]), lax.rem(iy + dy + grid[1], grid[1])),
        device_id_type=MESH,
    )


def rim_copies(grid, field, side, strip, send_sem, recv_sem):
    rows = field.shape[1]
    copies = [
        neighbour_copy(grid, 0, 1, field, side.at[0], send_sem.at[0], recv_sem.at[0]),
        neighbour_copy(grid, 0, -1, field, side.at[1], send_sem.at[1], recv_sem.at[1]),
    ]
    for k in range(3):
        dy = 1 - k
        copies.append(
            neighbour_copy(
                grid, 1, dy, field.at[:, pl.ds(rows - 8, 8), :], strip.at[k],
                send_sem.at[2 + k], recv_sem.at[2 + k],
            )
        )
    for k in range(3):
        dy = 1 - k
        copies.append(
            neighbour_copy(
                grid, -1, dy, field.at[:, pl.ds(0, 8), :], strip.at[3 + k],
                send_sem.at[5 + k], recv_sem.at[5 + k],
            )
        )
    return copies


def exchange_kernel(
    grid, pay, xu, xd, yu, yd, stat,
    pay_in, xu_in, xd_in, yu_in, yd_in, corner_in, side_in, strip_in,
    pay_send, pay_recv, lb_send, lb_recv, rim_send, rim_recv,
):
    ix, iy = position(grid)
    me = ix * grid[1] + iy
    greet_all(grid)
    to_all(grid, lambda o: pay.at[o], lambda m: pay_in.at[m], pay_send, pay_recv, True)
    nx = yu.shape[1]
    copies = rim_copies(grid, stat, side_in, strip_in, rim_send, rim_recv)
    plan = [
        (1, 0, xu, xu_in),
        (-1, 0, xd, xd_in),
        (0, 1, yu, yu_in),
        (0, -1, yd, yd_in),
    ]
    for k, q in enumerate(diagonal):
        dx, dy, _ = lattice_dirs[q]
        edge = yu.at[y_up.index(q)] if dy == 1 else yd.at[y_down.index(q)]
        plan.append((dx, dy, edge.at[nx - 1 if dx == 1 else 0], corner_in.at[k]))
    for number, (dx, dy, source, target) in enumerate(plan):
        copies.append(
            neighbour_copy(grid, dx, dy, source, target, lb_send.at[number], lb_recv.at[number])
        )
    for copy in copies:
        copy.start()
    pay_in[me] = pay[me]
    to_all(grid, lambda o: pay.at[o], lambda m: pay_in.at[m], pay_send, pay_recv, False)
    for copy in copies:
        copy.wait()


def exchange(grid, pay, xu, xd, yu, yd, stat):
    devices = grid[0] * grid[1]
    depth = xu.shape[2]
    shapes = [pay.shape, xu.shape, xd.shape, yu.shape, yd.shape, (4, 1, depth)]
    shapes += [(2,) + stat.shape, (6, stat.shape[0], 8, stat.shape[2])]
    vmem = pl.BlockSpec(memory_space=pltpu.VMEM)
    return pl.pallas_call(
        functools.partial(exchange_kernel, grid),
        in_specs=[vmem] * 6,
        out_specs=[vmem] * len(shapes),
        out_shape=[jax.ShapeDtypeStruct(shape, F32) for shape in shapes],
        scratch_shapes=[
            pltpu.SemaphoreType.DMA((devices,)),
            pltpu.SemaphoreType.DMA((devices,)),
            pltpu.SemaphoreType.DMA((8,)),
            pltpu.SemaphoreType.DMA((8,)),
            pltpu.SemaphoreType.DMA((8,)),
            pltpu.SemaphoreType.DMA((8,)),
        ],
        compiler_params=pltpu.CompilerParams(collective_id=0, has_side_effects=True),
        name="exchange",
    )(pay, xu, xd, yu, yd, stat)


def return_kernel(grid, pay, pay_in, pay_send, pay_recv):
    ix, iy = position(grid)
    me = ix * grid[1] + iy
    greet_all(grid)
    to_all(grid, lambda o: pay.at[o], lambda m: pay_in.at[m], pay_send, pay_recv, True)
    pay_in[me] = pay[me]
    to_all(grid, lambda o: pay.at[o], lambda m: pay_in.at[m], pay_send, pay_recv, False)


def send_back(grid, pay):
    devices = grid[0] * grid[1]
    vmem = pl.BlockSpec(memory_space=pltpu.VMEM)
    return pl.pallas_call(
        functools.partial(return_kernel, grid),
        in_specs=[vmem],
        out_specs=vmem,
        out_shape=jax.ShapeDtypeStruct(pay.shape, F32),
        scratch_shapes=[
            pltpu.SemaphoreType.DMA((devices,)),
            pltpu.SemaphoreType.DMA((devices,)),
        ],
        compiler_params=pltpu.CompilerParams(collective_id=2, has_side_effects=True),
        name="send_back",
    )(pay)


def joined(block, first, parts):
    return jnp.concatenate([block[first + p : first + p + 1] for p in range(parts)], axis=1)


def force_kernel(parts, pay_ref, force_ref):
    devices = pay_ref.shape[0]
    rows, cols = force_ref.shape[1:]
    width = parts * LANES

    def one(d, total):
        block = pay_ref[d]
        node = joined(block, 3 * parts, parts).astype(jnp.int32)
        row = node // cols
        col = node - row * cols
        row_hot = iota((rows, width), 0) == row
        col_hot = (iota((cols, width), 0) == col).astype(F32).astype(BF16)
        highs = []
        lows = []
        for c in range(3):
            value = joined(block, c * parts, parts)
            high = value.astype(BF16).astype(F32)
            highs.append(jnp.where(row_hot, high, 0.0))
            lows.append(jnp.where(row_hot, value - high, 0.0))
        left = jnp.concatenate(
            [jnp.concatenate(highs, axis=0).astype(BF16), jnp.concatenate(lows, axis=0).astype(BF16)],
            axis=1,
        )
        return total + dot_nt(left, jnp.concatenate([col_hot, col_hot], axis=1))

    total = lax.fori_loop(0, devices, one, jnp.zeros((3 * rows, cols), F32))
    for c in range(3):
        force_ref[c] = total[c * rows : (c + 1) * rows]


def force_of(parts, pay, rows, cols):
    return pl.pallas_call(
        functools.partial(force_kernel, parts),
        out_shape=jax.ShapeDtypeStruct((3, rows, cols), F32),
        name="force",
    )(pay)


def pick_kernel(parts, disp_ref, pay_ref, out_ref):
    devices = pay_ref.shape[0]
    rows, cols = disp_ref.shape[1:]
    width = parts * LANES
    high, low = halves(jnp.concatenate([disp_ref[c] for c in range(3)], axis=0))
    left = jnp.concatenate([high, low], axis=1)

    def one(d, carry):
        node = joined(pay_ref[d], 3 * parts, parts).astype(jnp.int32)
        row = node // cols
        col = node - row * cols
        row_hot = iota((rows, width), 0) == row
        col_hot = (iota((cols, width), 0) == col).astype(F32).astype(BF16)
        found = dot_nn(left, jnp.concatenate([col_hot, col_hot], axis=0))
        pieces = []
        for c in range(3):
            value = jnp.sum(
                jnp.where(row_hot, found[c * rows : (c + 1) * rows], 0.0), axis=0, keepdims=True
            )
            pieces += [value[:, p * LANES : (p + 1) * LANES] for p in range(parts)]
        pieces.append(jnp.zeros((8 - 3 * parts, LANES), F32))
        out_ref[d] = jnp.concatenate(pieces, axis=0)
        return carry

    lax.fori_loop(0, devices, one, 0)


def pick(parts, disp, pay):
    return pl.pallas_call(
        functools.partial(pick_kernel, parts),
        out_shape=jax.ShapeDtypeStruct(pay.shape, F32),
        name="pick",
    )(disp, pay)


def with_rim(centre, side, strip, c):
    rows, cols = centre.shape[1:]
    left_half = iota((rows, cols), 1) < cols // 2
    main = jnp.concatenate([centre[c], jnp.where(left_half, side[1, c], side[0, c])], axis=1)
    low = iota((8, cols), 0) < 4
    left_strip = iota((8, cols), 1) < cols // 2
    below = jnp.where(low, strip[4, c], strip[1, c])
    corner = jnp.where(
        low,
        jnp.where(left_strip, strip[5, c], strip[3, c]),
        jnp.where(left_strip, strip[2, c], strip[0, c]),
    )
    return jnp.concatenate([main, jnp.concatenate([below, corner], axis=1)], axis=0)


def solve_kernel(
    grid, stiff, force, stat, stat_side, stat_strip, disp,
    side, strip, one_buf, two_buf, rim_send, rim_recv, one_send, one_recv, two_send, two_recv,
):
    ix, iy = position(grid)
    me = ix * grid[1] + iy
    rows, cols = force.shape[1:]
    full = (rows + 8, 2 * cols)
    greet_all(grid)
    copies = rim_copies(grid, force, side, strip, rim_send, rim_recv)
    for copy in copies:
        copy.start()

    def back_row(a):
        return pltpu.roll(a, full[0] - 1, 0)

    def back_col(a):
        return pltpu.roll(a, full[1] - 1, 1)

    moduli = with_rim(stat, stat_side, stat_strip, 0)
    live = with_rim(stat, stat_side, stat_strip, 1)
    mass = with_rim(stat, stat_side, stat_strip, 2)
    next_row = back_row(moduli)
    scale = live * (moduli + next_row + back_col(moduli) + back_col(next_row)) * 0.25

    def operate(fields):
        down = [back_row(f) for f in fields]
        corners = (
            list(fields) + down + [back_col(f) for f in fields] + [back_col(f) for f in down]
        )
        results = []
        for k in range(12):
            total = stiff[k, 0] * corners[0]
            for l in range(1, 12):
                total = total + stiff[k, l] * corners[l]
            results.append(scale * total)
        images = []
        for c in range(3):
            right = results[6 + c] + pltpu.roll(results[9 + c], 1, 0)
            images.append(
                mass * fields[c]
                + results[c]
                + pltpu.roll(results[3 + c], 1, 0)
                + pltpu.roll(right, 1, 1)
            )
        return images

    def inner(a, b):
        total = a[0][:rows, :cols] * b[0][:rows, :cols]
        for c in range(1, 3):
            total = total + a[c][:rows, :cols] * b[c][:rows, :cols]
        return jnp.sum(jnp.sum(total, axis=0, keepdims=True), axis=1, keepdims=True)

    def sum_over_devices(values, buf, send_sem, recv_sem):
        lane = iota((1, LANES), 1)
        line = jnp.zeros((1, LANES), F32)
        for k, value in enumerate(values):
            line = jnp.where(lane == k, value, line)
        buf[me] = line
        source = lambda o: buf.at[me]
        target = lambda m: buf.at[m]
        to_all(grid, source, target, send_sem, recv_sem, True)
        to_all(grid, source, target, send_sem, recv_sem, False)
        total = jnp.sum(buf[...], axis=0)
        return [total[:, k : k + 1] for k in range(len(values))]

    for copy in copies:
        copy.wait()
    field = [with_rim(force, side, strip, c) for c in range(3)]
    image = operate(field)
    ff, fq = sum_over_devices(
        [inner(field, field), inner(field, image)], one_buf, one_send, one_recv
    )
    first = ff / fq
    residual = [field[c] - first * image[c] for c in range(3)]
    second_image = operate(residual)
    rr, rs, rq = sum_over_devices(
        [inner(residual, residual), inner(residual, second_image), inner(residual, image)],
        two_buf, two_send, two_recv,
    )
    ratio = rr / ff
    second = rr / (rs + 2.0 * ratio * rq + ratio * ratio * fq)
    for c in range(3):
        f = field[c][:rows, :cols]
        disp[c] = first * f + second * (residual[c][:rows, :cols] + ratio * f)


def solve(grid, stiff, force, stat, stat_side, stat_strip):
    devices = grid[0] * grid[1]
    vmem = pl.BlockSpec(memory_space=pltpu.VMEM)
    return pl.pallas_call(
        functools.partial(solve_kernel, grid),
        in_specs=[pl.BlockSpec(memory_space=pltpu.SMEM)] + [vmem] * 4,
        out_specs=vmem,
        out_shape=jax.ShapeDtypeStruct(force.shape, F32),
        scratch_shapes=[
            pltpu.VMEM((2,) + force.shape, F32),
            pltpu.VMEM((6, 3, 8, force.shape[2]), F32),
            pltpu.VMEM((devices, 1, LANES), F32),
            pltpu.VMEM((devices, 1, LANES), F32),
            pltpu.SemaphoreType.DMA((8,)),
            pltpu.SemaphoreType.DMA((8,)),
            pltpu.SemaphoreType.DMA((devices,)),
            pltpu.SemaphoreType.DMA((devices,)),
            pltpu.SemaphoreType.DMA((devices,)),
            pltpu.SemaphoreType.DMA((devices,)),
        ],
        compiler_params=pltpu.CompilerParams(collective_id=1, has_side_effects=True),
        name="solve",
    )(stiff, force, stat, stat_side, stat_strip)


def forcing_kernel(parts, back_ref, w_ref, blk_ref, own_ref, slot_ref, out_ref, back_cat):
    step = pl.program_id(0)
    devices = back_ref.shape[0]
    blocks = out_ref.shape[0] // 3
    chunk = w_ref.shape[0]

    @pl.when(step == 0)
    def _():
        high, low = halves(back_ref[...].reshape(devices * 8, LANES))
        back_cat[...] = jnp.concatenate([high, low], axis=1)
        out_ref[...] = jnp.zeros_like(out_ref)

    slot_id = slot_ref[...]
    part = slot_id // LANES
    place = slot_id - part * LANES
    slot_hot = (iota((LANES, chunk), 0) == place).astype(F32).astype(BF16)
    found = dot_nn(back_cat[...], jnp.concatenate([slot_hot, slot_hot], axis=0))
    mine = (iota((devices * 8, chunk), 0) // 8) == own_ref[...]
    lines = jnp.sum(jnp.where(mine, found, 0.0).reshape(devices, 8, chunk), axis=0)
    channel = iota((8, chunk), 0) // parts
    in_part = (iota((8, chunk), 0) - channel * parts) == part
    here = iota((blocks, chunk), 0) == blk_ref[...]
    highs = []
    lows = []
    for c in range(3):
        moved = coupling * jnp.sum(
            jnp.where(in_part & (channel == c), lines, 0.0), axis=0, keepdims=True
        )
        high = moved.astype(BF16).astype(F32)
        highs.append(jnp.where(here, high, 0.0).astype(BF16))
        lows.append(jnp.where(here, moved - high, 0.0).astype(BF16))
    high = jnp.concatenate(highs, axis=0)
    low = jnp.concatenate(lows, axis=0)
    w_high, w_low = halves(w_ref[...])
    out_ref[...] += dot_nn(
        jnp.concatenate([high, low, high], axis=1),
        jnp.concatenate([w_high, w_high, w_low], axis=0),
    )


def forcing_of(parts, blocks, back, weights, blk, own, slot):
    records, depth = weights.shape
    chunk = 512
    row_spec = pl.BlockSpec((1, chunk), lambda i: (0, i))
    return pl.pallas_call(
        functools.partial(forcing_kernel, parts),
        grid=(records // chunk,),
        in_specs=[
            pl.BlockSpec(back.shape, lambda i: (0, 0, 0)),
            pl.BlockSpec((chunk, depth), lambda i: (i, 0)),
            row_spec,
            row_spec,
            row_spec,
        ],
        out_specs=pl.BlockSpec((3 * blocks, depth), lambda i: (0, 0)),
        out_shape=jax.ShapeDtypeStruct((3 * blocks, depth), F32),
        scratch_shapes=[pltpu.VMEM((back.shape[0] * 8, 2 * LANES), BF16)],
        compiler_params=pltpu.CompilerParams(dimension_semantics=("arbitrary",)),
        name="forcing",
    )(back, weights, blk, own, slot)


def stream_kernel(
    cur, prev_ref, next_ref, forcing, xu, xd, yu, yd, yu_prev, yu_next, yd_prev, yd_next, corner,
    out_ref,
):
    step = pl.program_id(0)
    last = pl.num_programs(0) - 1
    rows, ny, nz = cur.shape[1:]
    fields = [forcing[c] for c in range(3)]

    def shifted(block, before, after, dx):
        if dx == 1:
            return jnp.concatenate([before[None], block[: rows - 1]], axis=0)
        if dx == -1:
            return jnp.concatenate([block[1:], after[None]], axis=0)
        return block

    for q in range(19):
        dx, dy, dz = lattice_dirs[q]
        before = after = None
        if dx == 1:
            before = jnp.where(step == 0, xu[x_up.index(q)], prev_ref[q, 0])
        if dx == -1:
            after = jnp.where(step == last, xd[x_down.index(q)], next_ref[q, 0])
        moved = shifted(cur[q], before, after, dx)
        if dy != 0:
            k = y_up.index(q) if dy == 1 else y_down.index(q)
            edge = (yu if dy == 1 else yd)[k]
            if dx == 1:
                before = (yu_prev if dy == 1 else yd_prev)[k, 0]
                before = jnp.where(step == 0, corner[diagonal.index(q)], before)
            if dx == -1:
                after = (yu_next if dy == 1 else yd_next)[k, 0]
                after = jnp.where(step == last, corner[diagonal.index(q)], after)
            edge = shifted(edge, before, after, dx)
            turned = pltpu.roll(moved, dy % ny, 1)
            at_edge = iota((rows, ny, nz), 1) == (0 if dy == 1 else ny - 1)
            moved = jnp.where(at_edge, jnp.broadcast_to(edge, (rows, ny, nz)), turned)
        if dz != 0:
            moved = pltpu.roll(moved, dz % nz, 2)
        projected = combine_dirs(fields, lattice_dirs[q])
        if projected is not None:
            moved = moved + (3.0 * lattice_weights[q]) * projected
        out_ref[q] = moved


def stream(relaxed, forcing, xu, xd, yu, yd, corner):
    _, nx, ny, nz = relaxed.shape
    rows = 4
    steps = nx // rows
    before = lambda i: (0, (i * rows + nx - 1) % nx, 0, 0)
    after = lambda i: (0, (i * rows + rows) % nx, 0, 0)
    whole3 = lambda i: (0, 0, 0)
    blocked = lambda i: (0, i, 0, 0)
    return pl.pallas_call(
        stream_kernel,
        grid=(steps,),
        in_specs=[
            pl.BlockSpec((19, rows, ny, nz), blocked),
            pl.BlockSpec((19, 1, ny, nz), before),
            pl.BlockSpec((19, 1, ny, nz), after),
            pl.BlockSpec((3, rows, ny, nz), blocked),
            pl.BlockSpec((5, ny, nz), whole3),
            pl.BlockSpec((5, ny, nz), whole3),
            pl.BlockSpec((5, rows, 1, nz), blocked),
            pl.BlockSpec((5, rows, 1, nz), blocked),
            pl.BlockSpec((5, 1, 1, nz), before),
            pl.BlockSpec((5, 1, 1, nz), after),
            pl.BlockSpec((5, 1, 1, nz), before),
            pl.BlockSpec((5, 1, 1, nz), after),
            pl.BlockSpec((4, 1, nz), whole3),
        ],
        out_specs=pl.BlockSpec((19, rows, ny, nz), blocked),
        out_shape=jax.ShapeDtypeStruct((19, nx, ny, nz), F32),
        compiler_params=pltpu.CompilerParams(dimension_semantics=("arbitrary",)),
        name="stream",
    )(relaxed, relaxed, relaxed, forcing, xu, xd, yu, yd, yu, yu, yd, yd, corner)


def per_device(
    grid, populations, mass, modulus, cell_live, stiff_ref, rec_block, rec_owner, rec_node,
    rbf_weight,
):
    devices = grid[0] * grid[1]
    _, nx, ny, nz = populations.shape
    records = rec_block.shape[0]
    rows, cols = mass.shape
    capacity = 2 * records // devices
    parts = -(-capacity // LANES)
    relaxed, moment, xu, xd, yu, yd = collide(populations)
    blk = rec_block.reshape(1, records)
    own = rec_owner.reshape(1, records)
    node = rec_node.reshape(1, records)
    stat = jnp.stack([modulus, cell_live.astype(F32), mass])
    pay, slot = pack_loads(
        devices, parts, cols, moment.reshape(3 * nx * ny, nz), rbf_weight, blk, own, node
    )
    pay, xu, xd, yu, yd, corner, side, strip = exchange(grid, pay, xu, xd, yu, yd, stat)
    force = force_of(parts, pay, rows, cols)
    displacement = solve(grid, stiff_ref, force, stat, side, strip)
    back = send_back(grid, pick(parts, displacement, pay))
    forcing = forcing_of(parts, nx * ny, back, rbf_weight, blk, own, slot)
    out = stream(relaxed, forcing.reshape(3, nx, ny, nz), xu, xd, yu, yd, corner)
    return out, displacement


def solution(mesh):
    grid = (mesh.shape["gx"], mesh.shape["gy"])
    in_specs = (
        P(None, "gx", "gy", None),
        P("gx", "gy"),
        P("gx", "gy"),
        P("gx", "gy"),
        P(),
        P(("gx", "gy")),
        P(("gx", "gy"), None),
        P(("gx", "gy")),
        P(("gx", "gy"), None),
    )
    out_specs = (P(None, "gx", "gy", None), P(None, "gx", "gy"))
    return jax.shard_map(
        functools.partial(per_device, grid), mesh=mesh, in_specs=in_specs, out_specs=out_specs,
        check_vma=False,
    )
```

profile of v0, /device:TPU:0, one launch (start us, length us, event | category | flops | bytes accessed | tf_op | source)
XLA Modules:
  0.0 112.0 jit_solution(5079803486190873768)
XLA Ops:
  0.6 0.8 convert_bitcast_fusion
  1.4 1.4 %pad_maximum_fusion.stat = f32[3,64,128]{2,1,0:T(8,128)} fusion(f32[1,64,128]{2,1,0:T(8,128)} %bitcast.15, f32[1,64,128]{2,1,0:T(8,128)S(1)} %convert_bitcast_fusion, f32[1,64,128]{2,1,0:T(8,128)} %bitcast.16), kind=kLoop, calls=%fused_computation | loop fusion | flops 49152 | bytes 196608 | tf_op jit(solution)/shard_map/stack | solution.py:789
  2.8 6.8 %collide.1 = (f32[19,32,8,256]{3,2,1,0:T(8,128)}, f32[3,32,8,256]{3,2,1,0:T(8,128)}, f32[5,8,256]{2,1,0:T(8,128)}, f32[5,8,256]{2,1,0:T(8,128)}, f32[5,32,1,256]{3,2,1,0:T(1,128)}, /*index=5*/f32[5,32,1,256]{3,2,1,0:T(1,128)}) custom-call(f32[19,32,8,256]{3,2,1,0:T(8,128)} %pop_ref.1), custom_call_target="tpu_custom_call" | custom-call | tf_op jit(solution)/shard_map/collide/pallas_call | solution.py:135
  9.6 12.3 %pack_loads.1 = (f32[32,8,128]{2,1,0:T(8,128)}, s32[1,4096]{1,0:T(1,128)}) custom-call(f32[768,256]{1,0:T(8,128)} %bitcast.10, f32[4096,256]{1,0:T(8,128)} %w_ref.3, s32[1,4096]{1,0:T(1,128)} %bitcast.11, s32[1,4096]{1,0:T(1,128)} %bitcast.13, s32[1,4096]{1,0:T(1,128)} %bitcast.17), custom_call_target="tpu_custom_call" | custom-call | tf_op jit(solution)/shard_map/pack_loads/pallas_call | solution.py:233
  21.9 19.4 %exchange.1 = (f32[32,8,128]{2,1,0:T(8,128)}, f32[5,8,256]{2,1,0:T(8,128)}, f32[5,8,256]{2,1,0:T(8,128)}, f32[5,32,1,256]{3,2,1,0:T(1,128)}, f32[5,32,1,256]{3,2...) custom-call(f32[32,8,128]{2,1,0:T(8,128)} %get-tuple-element.20.pay, ...), custom_call_target="tpu_custom_call" | custom-call | tf_op jit(solution)/shard_map/exchange/pallas_call | solution.py:387
  41.2 8.8 %force.1 = f32[3,64,128]{2,1,0:T(8,128)} custom-call(f32[32,8,128]{2,1,0:T(8,128)} %get-tuple-element.25.pay_ref), custom_call_target="tpu_custom_call" | custom-call | tf_op jit(solution)/shard_map/force/pallas_call | solution.py:466
  50.0 23.9 %solve.1.disp_ref = f32[3,64,128]{2,1,0:T(8,128)} custom-call(f32[12,12]{1,0:T(8,128)} %stiff.1, f32[3,64,128]{2,1,0:T(8,128)} %force.1, f32[3,64,128]{2,1,0:T(8,128)} %pad_maximum_fusion.stat, f32[2,3,64,128]{3,2,1,0:T(8,128)} %get-tuple-element.26.stat_side, f32[6,3,8,128]{3,2,1,0:T(8,128)} %get-tuple-element.27.stat_strip), custom_call_target="tpu_custom_call" | custom-call | tf_op jit(solution)/shard_map/solve/pallas_call | solution.py:613
  73.9 8.4 %pick.1.pay = f32[32,8,128]{2,1,0:T(8,128)} custom-call(f32[3,64,128]{2,1,0:T(8,128)} %solve.1.disp_ref, f32[32,8,128]{2,1,0:T(8,128)} %get-tuple-element.25.pay_ref), custom_call_target="tpu_custom_call" | custom-call | tf_op jit(solution)/shard_map/pick/pallas_call | solution.py:501
  82.3 10.4 %send_back.1.back_ref = f32[32,8,128]{2,1,0:T(8,128)} custom-call(f32[32,8,128]{2,1,0:T(8,128)} %pick.1.pay), custom_call_target="tpu_custom_call" | custom-call | tf_op jit(solution)/shard_map/send_back/pallas_call | solution.py:417
  92.7 10.4 %forcing.1 = f32[768,256]{1,0:T(8,128)} custom-call(f32[32,8,128]{2,1,0:T(8,128)} %send_back.1.back_ref, f32[4096,256]{1,0:T(8,128)} %w_ref.3, s32[1,4096]{1,0:T(1,128)} %bitcast.12, s32[1,4096]{1,0:T(1,128)} %bitcast.14, s32[1,4096]{1,0:T(1,128)} %get-tuple-element.28.slot_ref), custom_call_target="tpu_custom_call" | custom-call | tf_op jit(solution)/shard_map/forcing/pallas_call | solution.py:679
  103.1 0.0 copy-start
  103.1 8.2 %stream.1 = f32[19,32,8,256]{3,2,1,0:T(8,128)} custom-call(f32[19,32,8,256]{3,2,1,0:T(8,128)} %get-tuple-element.18.cur.prev_ref.next_ref, f32[19,32,8,256]{3,2,1,0:T(8,128)} %get-tuple-element.18.cur.prev_ref.next_ref, f32[19,32,8,256]{3,2,1,0:T(8,128)} %get-tuple-element.18.cur.prev_ref.next_ref, f32[3,32,8,256]{3,2,1,0:T(8,128)} %bitcast.9, ...), custom_call_target="tpu_custom_call" | custom-call | tf_op jit(solution)/shard_map/stream/pallas_call | solution.py:750
  111.4 0.0 copy-done
  111.4 0.6 copy.12
Async XLA Ops:
  103.1 8.2 %copy-start = (f32[3,64,128]{2,1,0:T(8,128)S(1)}, f32[3,64,128]{2,1,0:T(8,128)}, u32[]{:S(2)}) copy-start(f32[3,64,128]{2,1,0:T(8,128)} %solve.1.disp_ref) | copy-start | bytes 294916
where the time goes:
time: 113 us; the launch traced here: 112 us
  Pallas kernels  109 us (96%)
  other arithmetic  2.18 us (2%)
    pallas_call x1, Pallas kernels, solve(): pl.pallas_call(functools.partial(solve_kernel, grid), in_specs=[pl.BlockS...  23.9 us
    pallas_call x1, Pallas kernels, exchange(): pl.pallas_call(functools.partial(exchange_kernel, grid), in_specs=[vmem]...  19.4 us
    pallas_call x1, Pallas kernels, pack_loads(): pl.pallas_call(functools.partial(pack_kernel, devices, parts, node_cols),...  12.3 us
    pallas_call x1, Pallas kernels, send_back(): pl.pallas_call(functools.partial(return_kernel, grid), in_specs=[vmem], o...  10.4 us
    pallas_call x1, Pallas kernels, forcing_of(): pl.pallas_call(functools.partial(forcing_kernel, parts), grid=(records //...  10.4 us
    pallas_call x1, Pallas kernels, force_of(): pl.pallas_call(functools.partial(force_kernel, parts), out_shape=jax.Shap...  8.78 us
    pallas_call x1, Pallas kernels, pick(): pl.pallas_call(functools.partial(pick_kernel, parts), out_shape=jax.Shape...  8.36 us
    pallas_call x1, Pallas kernels, stream(): pl.pallas_call(stream_kernel, grid=(steps,), in_specs=[pl.BlockSpec((19,...  8.24 us

commit v1 on v0

--- a/solution.py
+++ b/solution.py
@@ -1,4 +1,5 @@
 import functools
+import math
 
 import jax
 import jax.numpy as jnp
@@ -345,164 +346,76 @@
     return copies
 
 
-def exchange_kernel(
-    grid, pay, xu, xd, yu, yd, stat,
-    pay_in, xu_in, xd_in, yu_in, yd_in, corner_in, side_in, strip_in,
-    pay_send, pay_recv, lb_send, lb_recv, rim_send, rim_recv,
-):
-    ix, iy = position(grid)
-    me = ix * grid[1] + iy
-    greet_all(grid)
-    to_all(grid, lambda o: pay.at[o], lambda m: pay_in.at[m], pay_send, pay_recv, True)
-    nx = yu.shape[1]
-    copies = rim_copies(grid, stat, side_in, strip_in, rim_send, rim_recv)
-    plan = [
-        (1, 0, xu, xu_in),
-        (-1, 0, xd, xd_in),
-        (0, 1, yu, yu_in),
-        (0, -1, yd, yd_in),
-    ]
-    for k, q in enumerate(diagonal):
-        dx, dy, _ = lattice_dirs[q]
-        edge = yu.at[y_up.index(q)] if dy == 1 else yd.at[y_down.index(q)]
-        plan.append((dx, dy, edge.at[nx - 1 if dx == 1 else 0], corner_in.at[k]))
-    for number, (dx, dy, source, target) in enumerate(plan):
-        copies.append(
-            neighbour_copy(grid, dx, dy, source, target, lb_send.at[number], lb_recv.at[number])
-        )
-    for copy in copies:
-        copy.start()
-    pay_in[me] = pay[me]
-    to_all(grid, lambda o: pay.at[o], lambda m: pay_in.at[m], pay_send, pay_recv, False)
-    for copy in copies:
-        copy.wait()
-
-
-def exchange(grid, pay, xu, xd, yu, yd, stat):
-    devices = grid[0] * grid[1]
-    depth = xu.shape[2]
-    shapes = [pay.shape, xu.shape, xd.shape, yu.shape, yd.shape, (4, 1, depth)]
-    shapes += [(2,) + stat.shape, (6, stat.shape[0], 8, stat.shape[2])]
-    vmem = pl.BlockSpec(memory_space=pltpu.VMEM)
-    return pl.pallas_call(
-        functools.partial(exchange_kernel, grid),
-        in_specs=[vmem] * 6,
-        out_specs=[vmem] * len(shapes),
-        out_shape=[jax.ShapeDtypeStruct(shape, F32) for shape in shapes],
-        scratch_shapes=[
-            pltpu.SemaphoreType.DMA((devices,)),
-            pltpu.SemaphoreType.DMA((devices,)),
-            pltpu.SemaphoreType.DMA((8,)),
-            pltpu.SemaphoreType.DMA((8,)),
-            pltpu.SemaphoreType.DMA((8,)),
-            pltpu.SemaphoreType.DMA((8,)),
-        ],
-        compiler_params=pltpu.CompilerParams(collective_id=0, has_side_effects=True),
-        name="exchange",
-    )(pay, xu, xd, yu, yd, stat)
-
-
-def return_kernel(grid, pay, pay_in, pay_send, pay_recv):
-    ix, iy = position(grid)
-    me = ix * grid[1] + iy
-    greet_all(grid)
-    to_all(grid, lambda o: pay.at[o], lambda m: pay_in.at[m], pay_send, pay_recv, True)
-    pay_in[me] = pay[me]
-    to_all(grid, lambda o: pay.at[o], lambda m: pay_in.at[m], pay_send, pay_recv, False)
-
-
-def send_back(grid, pay):
-    devices = grid[0] * grid[1]
-    vmem = pl.BlockSpec(memory_space=pltpu.VMEM)
-    return pl.pallas_call(
-        functools.partial(return_kernel, grid),
-        in_specs=[vmem],
-        out_specs=vmem,
-        out_shape=jax.ShapeDtypeStruct(pay.shape, F32),
-        scratch_shapes=[
-            pltpu.SemaphoreType.DMA((devices,)),
-            pltpu.SemaphoreType.DMA((devices,)),
-        ],
-        compiler_params=pltpu.CompilerParams(collective_id=2, has_side_effects=True),
-        name="send_back",
-    )(pay)
-
-
-def joined(block, first, parts):
-    return jnp.concatenate([block[first + p : first + p + 1] for p in range(parts)], axis=1)
-
-
-def force_kernel(parts, pay_ref, force_ref):
-    devices = pay_ref.shape[0]
-    rows, cols = force_ref.shape[1:]
-    width = parts * LANES
-
-    def one(d, total):
-        block = pay_ref[d]
-        node = joined(block, 3 * parts, parts).astype(jnp.int32)
-        row = node // cols
-        col = node - row * cols
-        row_hot = iota((rows, width), 0) == row
-        col_hot = (iota((cols, width), 0) == col).astype(F32).astype(BF16)
+def lines_of(ref, first, count, row, parts):
+    return jnp.concatenate(
+        [ref[first + d, row + p : row + p + 1] for d in range(count) for p in range(parts)],
+        axis=1,
+    )
+
+
+def node_hots(ref, first, count, parts, rows, cols):
+    node = lines_of(ref, first, count, 3 * parts, parts).astype(jnp.int32)
+    row = node // cols
+    col = node - row * cols
+    width = count * parts * LANES
+    row_hot = iota((rows, width), 0) == row
+    col_hot = (iota((cols, width), 0) == col).astype(F32).astype(BF16)
+    return row_hot, col_hot
+
+
+def gather_force(parts, pay, force):
+    devices = pay.shape[0]
+    rows, cols = force.shape[1:]
+    count = math.gcd(devices, 4)
+
+    def one(step, total):
+        first = step * count
+        row_hot, col_hot = node_hots(pay, first, count, parts, rows, cols)
         highs = []
         lows = []
         for c in range(3):
-            value = joined(block, c * parts, parts)
+            value = lines_of(pay, first, count, c * parts, parts)
             high = value.astype(BF16).astype(F32)
-            highs.append(jnp.where(row_hot, high, 0.0))
-            lows.append(jnp.where(row_hot, value - high, 0.0))
+            highs.append(jnp.where(row_hot, high, 0.0).astype(BF16))
+            lows.append(jnp.where(row_hot, value - high, 0.0).astype(BF16))
         left = jnp.concatenate(
-            [jnp.concatenate(highs, axis=0).astype(BF16), jnp.concatenate(lows, axis=0).astype(BF16)],
-            axis=1,
+            [jnp.concatenate(highs, axis=0), jnp.concatenate(lows, axis=0)], axis=1
         )
         return total + dot_nt(left, jnp.concatenate([col_hot, col_hot], axis=1))
 
-    total = lax.fori_loop(0, devices, one, jnp.zeros((3 * rows, cols), F32))
+    total = lax.fori_loop(0, devices // count, one, jnp.zeros((3 * rows, cols), F32))
     for c in range(3):
-        force_ref[c] = total[c * rows : (c + 1) * rows]
-
-
-def force_of(parts, pay, rows, cols):
-    return pl.pallas_call(
-        functools.partial(force_kernel, parts),
-        out_shape=jax.ShapeDtypeStruct((3, rows, cols), F32),
-        name="force",
-    )(pay)
-
-
-def pick_kernel(parts, disp_ref, pay_ref, out_ref):
-    devices = pay_ref.shape[0]
-    rows, cols = disp_ref.shape[1:]
-    width = parts * LANES
-    high, low = halves(jnp.concatenate([disp_ref[c] for c in range(3)], axis=0))
+        force[c] = total[c * rows : (c + 1) * rows]
+
+
+def pick_moved(parts, disp, pay, out):
+    devices = pay.shape[0]
+    rows, cols = disp[0].shape
+    count = math.gcd(devices, 4)
+    high, low = halves(jnp.concatenate(disp, axis=0))
     left = jnp.concatenate([high, low], axis=1)
 
-    def one(d, carry):
-        node = joined(pay_ref[d], 3 * parts, parts).astype(jnp.int32)
-        row = node // cols
-        col = node - row * cols
-        row_hot = iota((rows, width), 0) == row
-        col_hot = (iota((cols, width), 0) == col).astype(F32).astype(BF16)
+    def one(step, carry):
+        first = step * count
+        row_hot, col_hot = node_hots(pay, first, count, parts, rows, cols)
         found = dot_nn(left, jnp.concatenate([col_hot, col_hot], axis=0))
-        pieces = []
-        for c in range(3):
-            value = jnp.sum(
+        values = [
+            jnp.sum(
                 jnp.where(row_hot, found[c * rows : (c + 1) * rows], 0.0), axis=0, keepdims=True
             )
-            pieces += [value[:, p * LANES : (p + 1) * LANES] for p in range(parts)]
-        pieces.append(jnp.zeros((8 - 3 * parts, LANES), F32))
-        out_ref[d] = jnp.concatenate(pieces, axis=0)
+            for c in range(3)
+        ]
+        for d in range(count):
+            pieces = []
+            for value in values:
+                for p in range(parts):
+                    at = (d * parts + p) * LANES
+                    pieces.append(value[:, at : at + LANES])
+            pieces.append(jnp.zeros((8 - 3 * parts, LANES), F32))
+            out[first + d] = jnp.concatenate(pieces, axis=0)
         return carry
 
-    lax.fori_loop(0, devices, one, 0)
-
-
-def pick(parts, disp, pay):
-    return pl.pallas_call(
-        functools.partial(pick_kernel, parts),
-        out_shape=jax.ShapeDtypeStruct(pay.shape, F32),
-        name="pick",
-    )(disp, pay)
+    lax.fori_loop(0, devices // count, one, 0)
 
 
 def with_rim(centre, side, strip, c):
@@ -520,15 +433,43 @@
     return jnp.concatenate([main, jnp.concatenate([below, corner], axis=1)], axis=0)
 
 
-def solve_kernel(
-    grid, stiff, force, stat, stat_side, stat_strip, disp,
-    side, strip, one_buf, two_buf, rim_send, rim_recv, one_send, one_recv, two_send, two_recv,
+def couple_kernel(
+    grid, parts, stiff, pay, xu, xd, yu, yd, modulus_ref, live_ref, mass_ref,
+    disp, back_in, xu_in, xd_in, yu_in, yd_in, corner_in,
+    pay_in, back, stat, stat_side, stat_strip, force, side, strip, one_buf, two_buf,
+    pay_send, pay_recv, back_send, back_recv, lb_send, lb_recv,
+    stat_send, stat_recv, rim_send, rim_recv, one_send, one_recv, two_send, two_recv,
 ):
     ix, iy = position(grid)
     me = ix * grid[1] + iy
     rows, cols = force.shape[1:]
     full = (rows + 8, 2 * cols)
+    stat[0] = modulus_ref[...]
+    stat[1] = live_ref[...].astype(F32)
+    stat[2] = mass_ref[...]
     greet_all(grid)
+    to_all(grid, lambda o: pay.at[o], lambda m: pay_in.at[m], pay_send, pay_recv, True)
+    stat_copies = rim_copies(grid, stat, stat_side, stat_strip, stat_send, stat_recv)
+    nx = yu.shape[1]
+    plan = [
+        (1, 0, xu, xu_in),
+        (-1, 0, xd, xd_in),
+        (0, 1, yu, yu_in),
+        (0, -1, yd, yd_in),
+    ]
+    for k, q in enumerate(diagonal):
+        dx, dy, _ = lattice_dirs[q]
+        edge = yu.at[y_up.index(q)] if dy == 1 else yd.at[y_down.index(q)]
+        plan.append((dx, dy, edge.at[nx - 1 if dx == 1 else 0], corner_in.at[k]))
+    lb_copies = [
+        neighbour_copy(grid, dx, dy, source, target, lb_send.at[number], lb_recv.at[number])
+        for number, (dx, dy, source, target) in enumerate(plan)
+    ]
+    pay_in[me] = pay[me]
+    to_all(grid, lambda o: pay.at[o], lambda m: pay_in.at[m], pay_send, pay_recv, False)
+    for copy in stat_copies + lb_copies:
+        copy.start()
+    gather_force(parts, pay_in, force)
     copies = rim_copies(grid, force, side, strip, rim_send, rim_recv)
     for copy in copies:
         copy.start()
@@ -539,6 +480,8 @@
     def back_col(a):
         return pltpu.roll(a, full[1] - 1, 1)
 
+    for copy in stat_copies:
+        copy.wait()
     moduli = with_rim(stat, stat_side, stat_strip, 0)
     live = with_rim(stat, stat_side, stat_strip, 1)
     mass = with_rim(stat, stat_side, stat_strip, 2)
@@ -602,34 +545,48 @@
     )
     ratio = rr / ff
     second = rr / (rs + 2.0 * ratio * rq + ratio * ratio * fq)
+    moved = []
     for c in range(3):
         f = field[c][:rows, :cols]
-        disp[c] = first * f + second * (residual[c][:rows, :cols] + ratio * f)
-
-
-def solve(grid, stiff, force, stat, stat_side, stat_strip):
+        moved.append(first * f + second * (residual[c][:rows, :cols] + ratio * f))
+        disp[c] = moved[c]
+    pick_moved(parts, moved, pay_in, back)
+    to_all(grid, lambda o: back.at[o], lambda m: back_in.at[m], back_send, back_recv, True)
+    back_in[me] = back[me]
+    to_all(grid, lambda o: back.at[o], lambda m: back_in.at[m], back_send, back_recv, False)
+    for copy in lb_copies:
+        copy.wait()
+
+
+def couple(grid, parts, stiff, pay, xu, xd, yu, yd, modulus, live, mass):
     devices = grid[0] * grid[1]
+    depth = xu.shape[2]
+    patch = (3,) + mass.shape
+    shapes = [patch, pay.shape, xu.shape, xd.shape, yu.shape, yd.shape, (4, 1, depth)]
     vmem = pl.BlockSpec(memory_space=pltpu.VMEM)
+    rim = [pltpu.VMEM((2,) + patch, F32), pltpu.VMEM((6, 3, 8, patch[2]), F32)]
+    to_each = pltpu.SemaphoreType.DMA((devices,))
+    to_near = pltpu.SemaphoreType.DMA((8,))
     return pl.pallas_call(
-        functools.partial(solve_kernel, grid),
-        in_specs=[pl.BlockSpec(memory_space=pltpu.SMEM)] + [vmem] * 4,
-        out_specs=vmem,
-        out_shape=jax.ShapeDtypeStruct(force.shape, F32),
+        functools.partial(couple_kernel, grid, parts),
+        in_specs=[pl.BlockSpec(memory_space=pltpu.SMEM)] + [vmem] * 8,
+        out_specs=[vmem] * len(shapes),
+        out_shape=[jax.ShapeDtypeStruct(shape, F32) for shape in shapes],
         scratch_shapes=[
-            pltpu.VMEM((2,) + force.shape, F32),
-            pltpu.VMEM((6, 3, 8, force.shape[2]), F32),
+            pltpu.VMEM(pay.shape, F32),
+            pltpu.VMEM(pay.shape, F32),
+            pltpu.VMEM(patch, F32),
+            *rim,
+            pltpu.VMEM(patch, F32),
+            *rim,
             pltpu.VMEM((devices, 1, LANES), F32),
             pltpu.VMEM((devices, 1, LANES), F32),
-            pltpu.SemaphoreType.DMA((8,)),
-            pltpu.SemaphoreType.DMA((8,)),
-            pltpu.SemaphoreType.DMA((devices,)),
-            pltpu.SemaphoreType.DMA((devices,)),
-            pltpu.SemaphoreType.DMA((devices,)),
-            pltpu.SemaphoreType.DMA((devices,)),
-        ],
-        compiler_params=pltpu.CompilerParams(collective_id=1, has_side_effects=True),
-        name="solve",
-    )(stiff, force, stat, stat_side, stat_strip)
+            to_each, to_each, to_each, to_each, to_near, to_near,
+            to_near, to_near, to_near, to_near, to_each, to_each, to_each, to_each,
+        ],
+        compiler_params=pltpu.CompilerParams(collective_id=0, has_side_effects=True),
+        name="couple",
+    )(stiff, pay, xu, xd, yu, yd, modulus, live, mass)
 
 
 def forcing_kernel(parts, back_ref, w_ref, blk_ref, own_ref, slot_ref, out_ref, back_cat):
@@ -786,14 +743,12 @@
     blk = rec_block.reshape(1, records)
     own = rec_owner.reshape(1, records)
     node = rec_node.reshape(1, records)
-    stat = jnp.stack([modulus, cell_live.astype(F32), mass])
     pay, slot = pack_loads(
         devices, parts, cols, moment.reshape(3 * nx * ny, nz), rbf_weight, blk, own, node
     )
-    pay, xu, xd, yu, yd, corner, side, strip = exchange(grid, pay, xu, xd, yu, yd, stat)
-    force = force_of(parts, pay, rows, cols)
-    displacement = solve(grid, stiff_ref, force, stat, side, strip)
-    back = send_back(grid, pick(parts, displacement, pay))
+    displacement, back, xu, xd, yu, yd, corner = couple(
+        grid, parts, stiff_ref, pay, xu, xd, yu, yd, modulus, cell_live, mass
+    )
     forcing = forcing_of(parts, nx * ny, back, rbf_weight, blk, own, slot)
     out = stream(relaxed, forcing.reshape(3, nx, ny, nz), xu, xd, yu, yd, corner)
     return out, displacement

time: 113 us -> 87.2 us (0.77)
  Pallas kernels: 109 us -> 85.4 us
  other arithmetic: 2.18 us -> 0 us
    pallas_call x5 -> x1, Pallas kernels: 70.8 us -> 47.6 us  [couple(): pl.pallas_call(functools.partial(couple_kernel, grid, parts), in_specs=[p...]
    another operation x2 -> x0, other arithmetic: 2.18 us -> none  [per_device(): stat = jnp.stack([modulus, cell_live.astype(F32), mass])]
where the time goes in v1:
time: 87.2 us; the launch traced here: 86.6 us
  Pallas kernels  85.4 us (98%)
    pallas_call x1, Pallas kernels, couple(): pl.pallas_call(functools.partial(couple_kernel, grid, parts), in_specs=[p...  47.6 us
    pallas_call x1, Pallas kernels, pack_loads(): pl.pallas_call(functools.partial(pack_kernel, devices, parts, node_cols),...  12.3 us
    pallas_call x1, Pallas kernels, forcing_of(): pl.pallas_call(functools.partial(forcing_kernel, parts), grid=(records //...  10.4 us
    pallas_call x1, Pallas kernels, stream(): pl.pallas_call(stream_kernel, grid=(steps,), in_specs=[pl.BlockSpec((19,...  8.24 us
    pallas_call x1, Pallas kernels, collide(): pl.pallas_call(collide_kernel, grid=(steps,), in_specs=[pl.BlockSpec((19,...  6.79 us

profile of v1, /device:TPU:0, one launch (start us, length us, event | category | flops | bytes accessed | tf_op | source)
XLA Modules:
  0.0 86.6 jit_solution(10377992511178683623)
XLA Ops:
  0.6 6.8 %collide.1 = (f32[19,32,8,256]{3,2,1,0:T(8,128)}, f32[3,32,8,256]{3,2,1,0:T(8,128)}, f32[5,8,256]{2,1,0:T(8,128)}, f32[5,8,256]{2,1,0:T(8,128)}, f32[5,32,1,256]{3,2,1,0:T(1,128)}, /*index=5*/f32[5,32,1,256]{3,2,1,0:T(1,128)}) custom-call(f32[19,32,8,256]{3,2,1,0:T(8,128)} %pop_ref.1), custom_call_target="tpu_custom_call" | custom-call | tf_op jit(solution)/shard_map/collide/pallas_call | solution.py:136
  7.4 12.3 %pack_loads.1 = (f32[32,8,128]{2,1,0:T(8,128)}, s32[1,4096]{1,0:T(1,128)}) custom-call(f32[768,256]{1,0:T(8,128)} %bitcast.6, f32[4096,256]{1,0:T(8,128)} %w_ref.3, s32[1,4096]{1,0:T(1,128)} %bitcast.7, s32[1,4096]{1,0:T(1,128)} %bitcast.9, s32[1,4096]{1,0:T(1,128)} %bitcast.11), custom_call_target="tpu_custom_call" | custom-call | tf_op jit(solution)/shard_map/pack_loads/pallas_call | solution.py:234
  19.7 47.6 %couple.1 = (f32[3,64,128]{2,1,0:T(8,128)}, f32[32,8,128]{2,1,0:T(8,128)}, f32[5,8,256]{2,1,0:T(8,128)}, f32[5,8,256]{2,1,0:T(8,128)}, f32[5,32,1,256]{3,2,1,0:T...) custom-call(f32[12,12]{1,0:T(8,128)} %stiff.1, f32[32,8,128]{2,1,0:T(8,128)} %get-tuple-element.19.pay, ...), custom_call_target="tpu_custom_call" | custom-call | tf_op jit(solution)/shard_map/couple/pallas_call | solution.py:570
  67.3 10.4 %forcing.1 = f32[768,256]{1,0:T(8,128)} custom-call(f32[32,8,128]{2,1,0:T(8,128)} %get-tuple-element.24.back_ref, f32[4096,256]{1,0:T(8,128)} %w_ref.3, s32[1,4096]{1,0:T(1,128)} %bitcast.8, s32[1,4096]{1,0:T(1,128)} %bitcast.10, s32[1,4096]{1,0:T(1,128)} %get-tuple-element.25.slot_ref), custom_call_target="tpu_custom_call" | custom-call | tf_op jit(solution)/shard_map/forcing/pallas_call | solution.py:636
  77.8 0.0 copy-start
  77.8 8.2 %stream.1 = f32[19,32,8,256]{3,2,1,0:T(8,128)} custom-call(f32[19,32,8,256]{3,2,1,0:T(8,128)} %get-tuple-element.17.cur.prev_ref.next_ref, f32[19,32,8,256]{3,2,1,0:T(8,128)} %get-tuple-element.17.cur.prev_ref.next_ref, f32[19,32,8,256]{3,2,1,0:T(8,128)} %get-tuple-element.17.cur.prev_ref.next_ref, f32[3,32,8,256]{3,2,1,0:T(8,128)} %bitcast.5, ...), custom_call_target="tpu_custom_call" | custom-call | tf_op jit(solution)/shard_map/stream/pallas_call | solution.py:707
  86.0 0.0 copy-done
  86.0 0.6 copy.12
Async XLA Ops:
  77.8 8.2 %copy-start = (f32[3,64,128]{2,1,0:T(8,128)S(1)}, f32[3,64,128]{2,1,0:T(8,128)}, u32[]{:S(2)}) copy-start(f32[3,64,128]{2,1,0:T(8,128)} %get-tuple-element.35) | copy-start | bytes 294916

commit v2 on v1

--- a/solution.py
+++ b/solution.py
@@ -116,7 +116,7 @@
                 yd_ref[y_down.index(q), row] = relaxed[0:1]
         return carry
 
-    lax.fori_loop(0, rows, one, 0)
+    lax.fori_loop(0, rows, one, 0, unroll=2)
 
     @pl.when(step == 0)
     def _():
@@ -273,7 +273,7 @@
     def signal(j, carry):
         other = lax.rem(me + j, devices)
         pl.semaphore_signal(
-            barrier, inc=1, device_id=(other // grid[1], lax.rem(other, grid[1])),
+            barrier, inc=1, device_id=(lax.div(other, grid[1]), lax.rem(other, grid[1])),
             device_id_type=MESH,
         )
         return carry
@@ -292,7 +292,7 @@
         dst_ref=target(me),
         send_sem=send_sem.at[j],
         recv_sem=recv_sem.at[j],
-        device_id=(other // grid[1], lax.rem(other, grid[1])),
+        device_id=(lax.div(other, grid[1]), lax.rem(other, grid[1])),
         device_id_type=MESH,
     )
 
@@ -631,7 +631,7 @@
 
 def forcing_of(parts, blocks, back, weights, blk, own, slot):
     records, depth = weights.shape
-    chunk = 512
+    chunk = 1024
     row_spec = pl.BlockSpec((1, chunk), lambda i: (0, i))
     return pl.pallas_call(
         functools.partial(forcing_kernel, parts),
@@ -698,7 +698,7 @@
 
 def stream(relaxed, forcing, xu, xd, yu, yd, corner):
     _, nx, ny, nz = relaxed.shape
-    rows = 4
+    rows = 8
     steps = nx // rows
     before = lambda i: (0, (i * rows + nx - 1) % nx, 0, 0)
     after = lambda i: (0, (i * rows + rows) % nx, 0, 0)

time: 87.2 us -> 82.8 us (0.950)
  Pallas kernels: 85.4 us -> 81.2 us
    pallas_call x1, Pallas kernels: 8.24 us -> 5.98 us  [stream(): pl.pallas_call(stream_kernel, grid=(steps,), in_specs=[pl.BlockSpec((19,...]
    pallas_call x1, Pallas kernels: 10.4 us -> 9.04 us  [forcing_of(): pl.pallas_call(functools.partial(forcing_kernel, parts), grid=(records //...]
where the time goes in v2:
time: 82.8 us; the launch traced here: 82.5 us
  Pallas kernels  81.2 us (98%)
    pallas_call x1, Pallas kernels, couple(): pl.pallas_call(functools.partial(couple_kernel, grid, parts), in_specs=[p...  47.3 us
    pallas_call x1, Pallas kernels, pack_loads(): pl.pallas_call(functools.partial(pack_kernel, devices, parts, node_cols),...  12.3 us
    pallas_call x1, Pallas kernels, forcing_of(): pl.pallas_call(functools.partial(forcing_kernel, parts), grid=(records //...  9.04 us
    pallas_call x1, Pallas kernels, collide(): pl.pallas_call(collide_kernel, grid=(steps,), in_specs=[pl.BlockSpec((19,...  6.56 us
    pallas_call x1, Pallas kernels, stream(): pl.pallas_call(stream_kernel, grid=(steps,), in_specs=[pl.BlockSpec((19,...  5.98 us

profile of v2, /device:TPU:0, one launch (start us, length us, event | category | flops | bytes accessed | tf_op | source)
XLA Modules:
  0.0 82.5 jit_solution(4484112046393690956)
XLA Ops:
  0.6 6.6 %collide.1 = (f32[19,32,8,256]{3,2,1,0:T(8,128)}, f32[3,32,8,256]{3,2,1,0:T(8,128)}, f32[5,8,256]{2,1,0:T(8,128)}, f32[5,8,256]{2,1,0:T(8,128)}, f32[5,32,1,256]{3,2,1,0:T(1,128)}, /*index=5*/f32[5,32,1,256]{3,2,1,0:T(1,128)}) custom-call(f32[19,32,8,256]{3,2,1,0:T(8,128)} %pop_ref.1), custom_call_target="tpu_custom_call" | custom-call | tf_op jit(solution)/shard_map/collide/pallas_call | solution.py:136
  7.2 12.3 %pack_loads.1 = (f32[32,8,128]{2,1,0:T(8,128)}, s32[1,4096]{1,0:T(1,128)}) custom-call(f32[768,256]{1,0:T(8,128)} %bitcast.6, f32[4096,256]{1,0:T(8,128)} %w_ref.3, s32[1,4096]{1,0:T(1,128)} %bitcast.7, s32[1,4096]{1,0:T(1,128)} %bitcast.9, s32[1,4096]{1,0:T(1,128)} %bitcast.11), custom_call_target="tpu_custom_call" | custom-call | tf_op jit(solution)/shard_map/pack_loads/pallas_call | solution.py:234
  19.5 47.3 %couple.1 = (f32[3,64,128]{2,1,0:T(8,128)}, f32[32,8,128]{2,1,0:T(8,128)}, f32[5,8,256]{2,1,0:T(8,128)}, f32[5,8,256]{2,1,0:T(8,128)}, f32[5,32,1,256]{3,2,1,0:T...) custom-call(f32[12,12]{1,0:T(8,128)} %stiff.1, f32[32,8,128]{2,1,0:T(8,128)} %get-tuple-element.19.pay, ...), custom_call_target="tpu_custom_call" | custom-call | tf_op jit(solution)/shard_map/couple/pallas_call | solution.py:570
  66.8 9.0 %forcing.1 = f32[768,256]{1,0:T(8,128)} custom-call(f32[32,8,128]{2,1,0:T(8,128)} %get-tuple-element.24.back_ref, f32[4096,256]{1,0:T(8,128)} %w_ref.3, s32[1,4096]{1,0:T(1,128)} %bitcast.8, s32[1,4096]{1,0:T(1,128)} %bitcast.10, s32[1,4096]{1,0:T(1,128)} %get-tuple-element.25.slot_ref), custom_call_target="tpu_custom_call" | custom-call | tf_op jit(solution)/shard_map/forcing/pallas_call | solution.py:636
  75.9 0.0 copy-start
  75.9 6.0 %stream.1 = f32[19,32,8,256]{3,2,1,0:T(8,128)} custom-call(f32[19,32,8,256]{3,2,1,0:T(8,128)} %get-tuple-element.17.cur.prev_ref.next_ref, f32[19,32,8,256]{3,2,1,0:T(8,128)} %get-tuple-element.17.cur.prev_ref.next_ref, f32[19,32,8,256]{3,2,1,0:T(8,128)} %get-tuple-element.17.cur.prev_ref.next_ref, f32[3,32,8,256]{3,2,1,0:T(8,128)} %bitcast.5, ...), custom_call_target="tpu_custom_call" | custom-call | tf_op jit(solution)/shard_map/stream/pallas_call | solution.py:707
  81.8 0.0 copy-done
  81.9 0.6 copy.12
Async XLA Ops:
  75.9 6.0 %copy-start = (f32[3,64,128]{2,1,0:T(8,128)S(1)}, f32[3,64,128]{2,1,0:T(8,128)}, u32[]{:S(2)}) copy-start(f32[3,64,128]{2,1,0:T(8,128)} %get-tuple-element.35) | copy-start | bytes 294916
